TPU v7x, 32 devices: a whole 2x2x4 slice. The times are simulated.
32 devices in a mesh: terms: 8 (over z, y), sect: 4 (over x, core).
Axes of the slice: x: 2, y: 2, z: 4, core: 2. Of those that a mesh axis runs over, the one named last changes fastest.
Arguments:
- wavefunction: float32 [2, 512, 16, 512], P(None, 'sect'), may hold values from -6 to 6
- left_blocks: float32 [8, 2, 512, 128], P('terms', None, 'sect'), may hold values from -0.125 to 0.125
- right_operators: float32 [8, 2, 512, 512], P('terms'), may hold values from -0.1875 to 0.1875
- site_operators: float32 [8, 2, 16, 16], P('terms'), may hold values from -1 to 1
- term_charge: int32 [8], replicated, may hold values from 0 to 1
- source_terms: int32 [8, 3], replicated, may hold values from 0 to 7, all different within a row
- coupling: float32 [2, 8, 3], replicated, may hold values from -0.01953125 to 0.01953125
- owner: int32 [8], replicated, may hold values from 0 to 7, each once
Outputs:
- sigma: float32 [2, 512, 16, 512], P(None, 'sect', None, 'terms')
- new_right: float32 [8, 2, 512, 128], P('terms', None, 'sect')
Inputs may be any that keep to these rules, and one draw needn't show every extreme that they name: `source_terms`: each row names 3 different terms, and every term is named by some row. `owner`: each index along terms owns exactly one new term.
All inputs are finite; a program needn't handle non-finite values.
Results may differ from a plain program's by a relative error of at most 0.0003.
Values sent between devices are 32-bit elements; how exact they have to be, the bound alone decides.
A program may use at most 128 MiB of HBM per device.

v0:
```python
import functools

import jax
import jax.numpy as jnp
from jax import lax
from jax.experimental import pallas as pl
from jax.experimental.pallas import tpu as pltpu
from jax.sharding import PartitionSpec as P

LANES = 128


def split(value):
    high = value.astype(jnp.bfloat16)
    return high, (value - high.astype(jnp.float32)).astype(jnp.bfloat16)


def triple(former, latter, dims=(((1,), (0,)), ((), ()))):
    dot = functools.partial(lax.dot_general, dimension_numbers=dims, preferred_element_type=jnp.float32)
    return dot(former[0], latter[0]) + dot(former[0], latter[1]) + dot(former[1], latter[0])


def act_kernel(wave_ref, ops_ref, coef_ref, y_ref, high, low, mixed):
    groups, _, phys, rows, _ = y_ref.shape

    @pl.when(pl.program_id(0) == 0)
    def _():
        both = (ops_ref[0], ops_ref[1], ops_ref[0] + ops_ref[1])
        for j, value in enumerate(both):
            high[j], low[j] = split(value)

    re, im = wave_ref[0], wave_ref[1]
    t = [triple(split(v), (high[j], low[j])) for j, v in enumerate((re, im, re + im))]
    for j, value in enumerate((t[0] - t[1], t[2] - t[0] - t[1], t[2] - 2.0 * t[1])):
        for g in range(groups):
            mixed[j, g] = value[:, g * LANES : (g + 1) * LANES]

    def block(step, carry):
        g, r = step // (rows // 8), step % (rows // 8)
        base = pl.multiple_of(r * 8 * phys, 8 * phys)
        x = [[mixed[j, g, pl.ds(base + q, 8, stride=phys), :] for q in range(phys)] for j in range(3)]
        out = pl.ds(pl.multiple_of(r * 8, 8), 8)
        for p in range(phys):
            s = []
            for j in range(3):
                total = coef_ref[j, g, p, 0:1, :] * x[j][0]
                for q in range(1, phys):
                    total = total + coef_ref[j, g, p, q : q + 1, :] * x[j][q]
                s.append(total)
            y_ref[g, 0, p, out, :] = s[0] - s[1]
            y_ref[g, 1, p, out, :] = s[2] - s[0] - s[1]
        return carry

    lax.fori_loop(0, groups * (rows // 8), block, 0)


def act(wave, ops, coef, phys):
    _, flat, bond = wave.shape
    rows = flat // phys
    width = ops.shape[2]
    groups = width // LANES
    step = 32
    return pl.pallas_call(
        act_kernel,
        grid=(rows // step,),
        in_specs=[
            pl.BlockSpec((2, step * phys, bond), lambda i: (0, i, 0)),
            pl.BlockSpec((2, bond, width), lambda i: (0, 0, 0)),
            pl.BlockSpec(coef.shape, lambda i: (0, 0, 0, 0, 0)),
        ],
        out_specs=pl.BlockSpec((groups, 2, phys, step, LANES), lambda i: (0, 0, 0, i, 0)),
        out_shape=jax.ShapeDtypeStruct((groups, 2, phys, rows, LANES), jnp.float32),
        scratch_shapes=[
            pltpu.VMEM((3, bond, width), jnp.bfloat16),
            pltpu.VMEM((3, bond, width), jnp.bfloat16),
            pltpu.VMEM((3, groups, step * phys, LANES), jnp.float32),
        ],
        compiler_params=pltpu.CompilerParams(vmem_limit_bytes=60 * 1024 * 1024),
    )(wave, ops, coef)


def close_kernel(charge_ref, y_ref, left_ref, local_ref, stay_ref, up_ref, gram_ref, high, low):
    per = left_ref.shape[0]
    phys = y_ref.shape[2]
    cols = LANES // per
    group = pl.program_id(0)

    @pl.when(group == 0)
    def _():
        high[...], low[...] = split(local_ref[...])
        stay_ref[...] = jnp.zeros_like(stay_ref)
        up_ref[...] = jnp.zeros_like(up_ref)

    for j in range(per):
        y = jnp.concatenate(
            [
                jnp.concatenate([y_ref[0, h, p, :, j * cols : (j + 1) * cols] for p in range(phys)], axis=1)
                for h in range(2)
            ],
            axis=0,
        )
        y = split(y)
        gram_ref[j] = triple(y, (high[...], low[...]), (((1,), (1,)), ((), ())))
        c = triple(split(left_ref[j]), y)
        raised = (charge_ref[group * per + j] == 1).astype(jnp.float32)
        up_ref[...] += c * raised
        stay_ref[...] += c * (1.0 - raised)


def close(charge, y, left, local):
    groups, _, phys, rows, _ = y.shape
    terms, tall, _ = left.shape
    per = terms // groups
    wide = local.shape[1]
    fixed = pl.BlockSpec((tall, wide), lambda i: (0, 0))
    return pl.pallas_call(
        close_kernel,
        grid=(groups,),
        in_specs=[
            pl.BlockSpec(memory_space=pltpu.SMEM),
            pl.BlockSpec((1, 2, phys, rows, LANES), lambda i: (i, 0, 0, 0, 0)),
            pl.BlockSpec((per, tall, tall), lambda i: (i, 0, 0)),
            fixed,
        ],
        out_specs=[fixed, fixed, pl.BlockSpec((per, tall, tall), lambda i: (i, 0, 0))],
        out_shape=[
            jax.ShapeDtypeStruct((tall, wide), jnp.float32),
            jax.ShapeDtypeStruct((tall, wide), jnp.float32),
            jax.ShapeDtypeStruct((terms, tall, tall), jnp.float32),
        ],
        scratch_shapes=[pltpu.VMEM((tall, wide), jnp.bfloat16)] * 2,
        compiler_params=pltpu.CompilerParams(vmem_limit_bytes=60 * 1024 * 1024),
    )(charge, y, left, local)

HIGH = lax.Precision.HIGH


def ein(pattern, former, latter, precision=HIGH):
    return jnp.einsum(pattern, former, latter, precision=precision, preferred_element_type=jnp.float32)


def body(wave, left, right, site, charge, source, coupling, owner):
    _, rows, phys, bond = wave.shape
    terms = lax.axis_size("terms")
    bands = lax.axis_size("sect")
    me = lax.axis_index("terms")
    band = lax.axis_index("sect")
    cols = bond // terms
    part = bond // bands
    mine = lax.dynamic_slice_in_dim(right[0], band * part, part, axis=1)
    mine = lax.all_to_all(mine.reshape(2, part, terms, cols), "terms", 2, 2, tiled=True)
    ops = lax.all_gather(mine, "sect", axis=1, tiled=True)
    ops = ops.reshape(2, bond, terms * cols)
    lefts = lax.all_gather(left, "terms", axis=0, tiled=True)
    sites = lax.all_gather(site, "terms", axis=0, tiled=True)
    weights = jnp.stack((sites[:, 0], sites[:, 1], sites[:, 0] + sites[:, 1]))
    coef = jnp.repeat(weights.transpose(0, 2, 3, 1), cols, axis=3)
    coef = coef.reshape(3, phys, phys, -1, LANES).transpose(0, 3, 1, 2, 4)
    y = act(wave.reshape(2, rows * phys, bond), ops, coef, phys)
    l_re, l_im = lefts[:, 0], lefts[:, 1]
    l = jnp.concatenate((jnp.concatenate((l_re, -l_im), 2), jnp.concatenate((l_im, l_re), 2)), 1)
    local = lax.dynamic_slice_in_dim(wave, me * cols, cols, axis=3).reshape(2 * rows, phys * cols)
    stay, up, g = close(charge, y, l, local)
    moved = lax.ppermute(up, "sect", [(i, i + 1) for i in range(bands - 1)])
    sigma = (stay + moved).reshape(2, rows, phys, cols)
    g = g.reshape(terms, 2, rows, 2, rows)
    q_re = g[:, 0, :, 0] + g[:, 1, :, 1]
    q_im = g[:, 1, :, 0] - g[:, 0, :, 1]
    term_ids = jnp.arange(terms, dtype=jnp.int32)
    hit = (source[:, :, None] == term_ids).astype(jnp.float32)
    place = (owner[None, :] == term_ids[:, None]).astype(jnp.float32)
    top = lax.Precision.HIGHEST
    w_re = ein("gj,jk->gk", place, ein("jt,jtk->jk", coupling[0], hit, top), top)
    w_im = ein("gj,jk->gk", place, ein("jt,jtk->jk", coupling[1], hit, top), top)
    n_re = ein("gk,kae->gae", w_re, q_re) - ein("gk,kae->gae", w_im, q_im)
    n_im = ein("gk,kae->gae", w_re, q_im) + ein("gk,kae->gae", w_im, q_re)
    new = lax.psum_scatter(jnp.stack((n_re, n_im), 1), "terms", scatter_dimension=0, tiled=True)
    return sigma, new


def solution(mesh):
    placed = (
        P(None, "sect", None, None),
        P("terms", None, "sect", None),
        P("terms", None, None, None),
        P("terms", None, None, None),
        P(),
        P(),
        P(),
        P(),
    )
    return jax.shard_map(
        body,
        mesh=mesh,
        in_specs=placed,
        out_specs=(P(None, "sect", None, "terms"), P("terms", None, "sect", None)),
        check_vma=False,
    )
```

profile of v0, /device:TPU:12, one launch (start us, length us, event | category | flops | bytes accessed | tf_op | source)
XLA Modules:
  0.0 216.9 jit_solution(11200702929547431992)
XLA Ops:
  7.2 0.7 all-gather.5.cloned.1.call-update
  8.0 0.8 copy-done
  9.1 22.3 %all_to_all.5 = f32[2,128,8,64]{1,3,0,2:T(8,128)S(1)} all-to-all(f32[2,128,8,64]{1,3,0,2:T(8,128)S(1)} %copy.37), channel_id=1, replica_groups=mesh['terms'=8,'sect'=4] {'terms'}, dimensions={2} | all-to-all | bytes 1048576 | tf_op jit(solution)/shard_map/all_to_all | solution.py:151
  31.4 0.9 copy.38
  32.3 27.4 %all_gather.10 = f32[8,2,16,16]{3,2,1,0:T(8,128)S(1)} all-gather(f32[1,2,16,16]{3,2,1,0:T(8,128)S(1)} %copy-done.1), channel_id=1, replica_groups=mesh['terms'=8,'sect'=4] {'terms'}, dimensions={0}, use_global_device_ids=true | all-gather | bytes 18432 | tf_op jit(solution)/shard_map/all_gather | solution.py:155
  60.0 2.2 broadcast_in_dim.2
  62.1 4.0 %reshape_reshape.3 = f32[3,16,16,4,128]{4,3,2,1,0:T(4,128)} reshape(f32[3,16,16,8,64]{4,3,2,1,0:T(8,128)} %broadcast_in_dim.2) | data formatting | bytes 3145728 | tf_op jit(solution)/shard_map/reshape;reshape | solution.py:158
  66.1 2.7 %copy.86 = f32[3,16,16,4,128]{4,2,1,3,0:T(8,128)} copy(f32[3,16,16,4,128]{4,3,2,1,0:T(4,128)} %reshape_reshape.3) | data formatting | bytes 3145728 | tf_op jit(solution)/shard_map/reshape;reshape | solution.py:158
  68.9 3.5 %constant_dynamic-slice_fusion = f32[2,128,16,64]{3,2,1,0:T(8,128)} fusion(f32[2,128,16,512]{3,2,1,0:T(8,128)} %param.8, s32[]{:T(128)S(6)} %select_n.7), kind=kLoop, calls=%fused_computation.28 | loop fusion | bytes 2097156 | tf_op jit(solution)/shard_map/dynamic_slice | solution.py:162
  72.4 2.8 %reshape.57.local_ref = f32[256,1024]{1,0:T(8,128)} reshape(f32[2,128,16,64]{3,2,1,0:T(8,128)} %constant_dynamic-slice_fusion) | data formatting | bytes 2097152 | tf_op jit(solution)/shard_map/reshape | solution.py:162
  75.5 0.2 fusion.11
  75.8 0.2 fusion.10
  76.2 1.1 fusion.17
  77.3 1.3 slice_bitcast_fusion
  78.5 1.6 maximum_maximum_fusion.left_ref
  80.1 2.9 %copy.42.ops_ref = f32[2,512,512]{2,1,0:T(8,128)} copy(f32[2,512,512]{1,2,0:T(8,128)} %bitcast.61) | data formatting | bytes 4194304 | tf_op jit(solution)/shard_map/reshape | solution.py:153
  83.0 34.9 %shard_map.95.y_ref = f32[4,2,16,128,128]{4,3,2,1,0:T(8,128)} custom-call(f32[2,2048,512]{2,1,0:T(8,128)} %bitcast.59, f32[2,512,512]{2,1,0:T(8,128)} %copy.42.ops_ref, f32[3,4,16,16,128]{4,3,2,1,0:T(8,128)} %bitcast.60), custom_call_target="tpu_custom_call" | custom-call | tf_op jit(solution)/shard_map/pallas_call | solution.py:63
  117.9 12.0 %shard_map.96 = (f32[256,1024]{1,0:T(8,128)}, f32[256,1024]{1,0:T(8,128)}, f32[8,256,256]{2,1,0:T(8,128)}) custom-call(s32[8]{0:T(128)} %charge_ref.1, f32[4,2,16,128,128]{4,3,2,1,0:T(8,128)} %shard_map.95.y_ref, f32[8,256,256]{2,1,0:T(8,128)} %maximum_maximum_fusion.left_ref, f32[256,1024]{1,0:T(8,128)} %reshape.57.local_ref), custom_call_target="tpu_custom_call" | custom-call | tf_op jit(solution)/shard_map/pallas_call | solution.py:116
  129.9 3.3 %reshape.50 = f32[8,2,128,2,128]{4,3,2,1,0:T(2,128)} reshape(f32[8,256,256]{2,1,0:T(8,128)} %get-tuple-element.7) | data formatting | bytes 4194304 | tf_op jit(solution)/shard_map/reshape | solution.py:166
  133.2 4.5 %fusion.18 = (f32[8,1,128,1,128]{4,3,2,1,0:T(1,128)S(1)}, f32[8,1,128,1,128]{4,3,2,1,0:T(1,128)S(1)}, f32[8,1,128,1,128]{4,3,2,1,0:T(1,128)S(1)}, f32[8,1,128,1,128]{4,3,2,1,0:T(1,128)S(1)}) fusion(f32[8,2,128,2,128]{4,3,2,1,0:T(2,128)} %reshape.50), kind=kLoop, calls=%fused_computation.32 | loop fusion | bytes 4194304 | tf_op jit(solution)/shard_map/slice | solution.py:167
  137.7 0.9 fusion.5
  138.6 0.9 fusion.7
  139.5 0.9 fusion.1
  140.4 0.9 fusion
  141.4 1.2 copy.52
  142.6 0.3 copy-done.5
  142.8 1.3 collective-permute-start
  144.2 2.2 %collective-permute-done = f32[256,1024]{1,0:T(8,128)S(1)} collective-permute-done((f32[256,1024]{1,0:T(8,128)S(1)}, f32[256,1024]{1,0:T(8,128)S(1)}, u32[]{:S(2)}, u32[]{:S(2)}) %collective-permute-start) | collective-permute-done | bytes 1048608 | tf_op jit(solution)/shard_map/ppermute | solution.py:164
  146.4 1.4 add.33
  147.8 1.9 reshape.58
  149.7 3.3 %copy.53 = f32[2,128,16,64]{1,3,2,0:T(8,128)} copy(f32[2,128,16,64]{3,2,1,0:T(8,128)} %reshape.58) | data formatting | bytes 2097152
  152.9 57.4 %reduce-scatter.2.cloned.1.call-done = f32[1,2,128,128]{3,2,1,0:T(8,128)} async-done(((f32[8,2,128,128]{3,2,1,0:T(8,128)}), f32[1,2,128,128]{3,2,1,0:T(8,128)}) %reduce-scatter.2.cloned.1.call-update) | async-done | bytes 131088 | tf_op jit(solution)/shard_map/reduce_scatter | solution.py:177
  (31 shorter events, 1.2 us)
Async XLA Ops:
  7.2 1.6 copy-start
  7.2 69.0 %all-gather.5.cloned.1.call-start = ((), (), s32[]{:S(2)}) async-start(), calls=%async_computation.3 | async-start | bytes 1179648 | tf_op jit(solution)/shard_map/all_gather | solution.py:154
  7.9 72.2 %all-gather.3.cloned.1.call-start = ((), (), s32[]{:S(2)}) async-start(), calls=%async_computation.2 | async-start | bytes 2621440 | tf_op jit(solution)/shard_map/all_gather | solution.py:152
  9.0 23.3 %copy-start.1 = (f32[1,2,16,16]{3,2,1,0:T(8,128)S(1)}, f32[1,2,16,16]{3,2,1,0:T(8,128)}, u32[]{:S(2)}) copy-start(f32[1,2,16,16]{3,2,1,0:T(8,128)} %param.11) | copy-start | bytes 6148
  32.3 178.1 %reduce-scatter.2.cloned.1.call-start = ((), (), s32[]{:S(2)}) async-start(), calls=%async_computation.4 | async-start | bytes 1179648 | tf_op jit(solution)/shard_map/reduce_scatter | solution.py:177
  72.4 2.8 %copy-start.2 = (f32[2,8,3]{1,0,2:T(2,128)S(1)}, f32[2,8,3]{1,0,2:T(2,128)}, u32[]{:S(2)}) copy-start(f32[2,8,3]{1,0,2:T(2,128)} %param.14) | copy-start | bytes 580
  72.4 2.9 %copy-start.3 = (s32[8,3]{0,1:T(4,128)S(1)}, s32[8,3]{0,1:T(4,128)}, u32[]{:S(2)}) copy-start(s32[8,3]{0,1:T(4,128)} %param.13) | copy-start | bytes 292
  72.4 3.3 %copy-start.4 = (s32[8]{0:T(128)S(1)}, s32[8]{0:T(128)}, u32[]{:S(2)}) copy-start(s32[8]{0:T(128)} %param.15) | copy-start | bytes 100
  141.4 1.5 copy-start.5
  142.8 3.6 %collective-permute-start = (f32[256,1024]{1,0:T(8,128)S(1)}, f32[256,1024]{1,0:T(8,128)S(1)}, u32[]{:S(2)}, u32[]{:S(2)}) collective-permute-start(f32[256,1024]{1,0:T(8,128)S(1)} %copy-done.5), channel_id=1, source_target_pairs={{0,1},{1,2},{2,3},{4,5},{5,6},{6,7},{8,9},{9,10},{10,11},{12,13},{... | collective-permute-start | bytes 3145736 | tf_op jit(solution)/shard_map/ppermute | solution.py:164
Sparse Core Ops, SparseCore 0:
  10.2 42.5 all-gather.4
  54.3 23.3 all-gather.2
  142.7 67.5 reduce-scatter.1
where the time goes:
time: 219 us; the launch traced here: 217 us
  waiting for transfers between devices  60.3 us (28%)
  blocking collectives  49.7 us (23%)
  Pallas kernels  46.9 us (21%)
  local copies, waits for them, and re-layouts  36.2 us (17%)
  between operations  13.9 us (6%)
  matrix products  4.23 us (2%)
  other arithmetic  4.12 us (2%)
    reduce_scatter x1, waiting for transfers between devices, body(): lax.psum_scatter(jnp.stack((n_re, n_im), 1), 'terms', scatter_dimension=0...  57.4 us
    pallas_call x1, Pallas kernels, act(): pl.pallas_call(act_kernel, grid=(rows // step,), in_specs=[pl.BlockSpec((...  34.9 us
    all_gather x1, blocking collectives, body(): sites = lax.all_gather(site, 'terms', axis=0, tiled=True)  27.4 us
    all_to_all x1, blocking collectives, body(): lax.all_to_all(mine.reshape(2, part, terms, cols), 'terms', 2, 2, tiled=T...  22.3 us
    pallas_call x1, Pallas kernels, close(): pl.pallas_call(close_kernel, grid=(groups,), in_specs=[pl.BlockSpec(memor...  12 us
    another operation x2, local copies, waits for them, and re-layouts, body(): coef = coef.reshape(3, phys, phys, -1, LANES).transpose(0, 3, 1, 2, 4)  6.75 us
    unnamed x15, local copies, waits for them, and re-layouts  4.64 us
    slice x1, local copies, waits for them, and re-layouts, body(): q_re = g[:, 0, :, 0] + g[:, 1, :, 1]  4.54 us
  transfers between devices with their start and end apart: 4, of which 2 were waited for; matrix products, arithmetic and copies ran while one was open for 13% of the time, Pallas kernels for 0%

commit v1 on v0

v1 whole, which is shorter than its diff:
```python
import functools

import jax
import jax.numpy as jnp
from jax import lax
from jax.experimental import pallas as pl
from jax.experimental.pallas import tpu as pltpu
from jax.sharding import PartitionSpec as P

LANES = 128


def split(value):
    high = value.astype(jnp.bfloat16)
    return high, (value - high.astype(jnp.float32)).astype(jnp.bfloat16)


def triple(former, latter, dims=(((1,), (0,)), ((), ()))):
    dot = functools.partial(lax.dot_general, dimension_numbers=dims, preferred_element_type=jnp.float32)
    return dot(former[0], latter[0]) + dot(former[0], latter[1]) + dot(former[1], latter[0])


def act_kernel(wave_ref, ops_ref, coef_ref, y_ref, high, low, mixed):
    groups, _, phys, rows, _ = y_ref.shape

    @pl.when(pl.program_id(0) == 0)
    def _():
        per = ops_ref.shape[0] // groups
        cols = LANES // per
        deep = ops_ref.shape[2]
        for g in range(groups):
            lanes = slice(g * LANES, (g + 1) * LANES)
            for i in range(per):
                part = [
                    jnp.concatenate(
                        [ops_ref[g * per + j, h, :, i * cols : (i + 1) * cols] for j in range(per)], axis=1
                    )
                    for h in range(2)
                ]
                for j, value in enumerate((part[0], part[1], part[0] + part[1])):
                    spot = (j, slice(i * deep, (i + 1) * deep), lanes)
                    high[spot], low[spot] = split(value)

    re, im = wave_ref[0], wave_ref[1]
    t = [triple(split(v), (high[j], low[j])) for j, v in enumerate((re, im, re + im))]
    for j, value in enumerate((t[0] - t[1], t[2] - t[0] - t[1], t[2] - 2.0 * t[1])):
        for g in range(groups):
            mixed[j, g] = value[:, g * LANES : (g + 1) * LANES]

    def block(step, carry):
        g, r = step // (rows // 8), step % (rows // 8)
        base = pl.multiple_of(r * 8 * phys, 8 * phys)
        x = [[mixed[j, g, pl.ds(base + q, 8, stride=phys), :] for q in range(phys)] for j in range(3)]
        out = pl.ds(pl.multiple_of(r * 8, 8), 8)
        for p in range(phys):
            s = []
            for j in range(3):
                total = coef_ref[j, g, p, 0:1, :] * x[j][0]
                for q in range(1, phys):
                    total = total + coef_ref[j, g, p, q : q + 1, :] * x[j][q]
                s.append(total)
            y_ref[g, 0, p, out, :] = s[0] - s[1]
            y_ref[g, 1, p, out, :] = s[2] - s[0] - s[1]
        return carry

    lax.fori_loop(0, groups * (rows // 8), block, 0)


def act(wave, ops, coef, phys):
    _, flat, bond = wave.shape
    rows = flat // phys
    groups = coef.shape[1]
    width = groups * LANES
    step = 32
    return pl.pallas_call(
        act_kernel,
        grid=(rows // step,),
        in_specs=[
            pl.BlockSpec((2, step * phys, bond), lambda i: (0, i, 0)),
            pl.BlockSpec(ops.shape, lambda i: (0, 0, 0, 0)),
            pl.BlockSpec(coef.shape, lambda i: (0, 0, 0, 0, 0)),
        ],
        out_specs=pl.BlockSpec((groups, 2, phys, step, LANES), lambda i: (0, 0, 0, i, 0)),
        out_shape=jax.ShapeDtypeStruct((groups, 2, phys, rows, LANES), jnp.float32),
        scratch_shapes=[
            pltpu.VMEM((3, bond, width), jnp.bfloat16),
            pltpu.VMEM((3, bond, width), jnp.bfloat16),
            pltpu.VMEM((3, groups, step * phys, LANES), jnp.float32),
        ],
        compiler_params=pltpu.CompilerParams(vmem_limit_bytes=60 * 1024 * 1024),
    )(wave, ops, coef)


def close_kernel(charge_ref, weight_ref, y_ref, left_ref, local_ref, stay_ref, up_ref, new_ref, high, low):
    per = left_ref.shape[0]
    terms = new_ref.shape[0]
    phys, rows = y_ref.shape[2], y_ref.shape[3]
    cols = LANES // per
    group = pl.program_id(0)

    @pl.when(group == 0)
    def _():
        high[...], low[...] = split(local_ref[...])
        stay_ref[...] = jnp.zeros_like(stay_ref)
        up_ref[...] = jnp.zeros_like(up_ref)
        new_ref[...] = jnp.zeros_like(new_ref)

    for j in range(per):
        term = group * per + j
        y = jnp.concatenate(
            [
                jnp.concatenate([y_ref[0, h, p, :, j * cols : (j + 1) * cols] for p in range(phys)], axis=1)
                for h in range(2)
            ],
            axis=0,
        )
        y = split(y)
        re, im = left_ref[j, :rows], left_ref[j, rows : 2 * rows]
        left = jnp.concatenate(
            [jnp.concatenate([re, -im], axis=1), jnp.concatenate([im, re], axis=1)], axis=0
        )
        c = triple(split(left), y)
        raised = (charge_ref[term] == 1).astype(jnp.float32)
        up_ref[...] += c * raised
        stay_ref[...] += c * (1.0 - raised)
        gram = triple(y, (high[...], low[...]), (((1,), (1,)), ((), ())))
        q_re = gram[:rows, :rows] + gram[rows:, rows:]
        q_im = gram[rows:, :rows] - gram[:rows, rows:]

        def add(g, carry):
            w_re, w_im = weight_ref[0, g, term], weight_ref[1, g, term]
            new_ref[g, :rows, :] += w_re * q_re - w_im * q_im
            new_ref[g, rows:, :] += w_re * q_im + w_im * q_re
            return carry

        lax.fori_loop(0, terms, add, 0)


def close(charge, weight, y, left, local):
    groups, _, phys, rows, _ = y.shape
    terms, lines, _ = left.shape
    per = terms // groups
    tall, wide = local.shape
    fixed = pl.BlockSpec((tall, wide), lambda i: (0, 0))
    return pl.pallas_call(
        close_kernel,
        grid=(groups,),
        in_specs=[
            pl.BlockSpec(memory_space=pltpu.SMEM),
            pl.BlockSpec(memory_space=pltpu.SMEM),
            pl.BlockSpec((1, 2, phys, rows, LANES), lambda i: (i, 0, 0, 0, 0)),
            pl.BlockSpec((per, lines, rows), lambda i: (i, 0, 0)),
            fixed,
        ],
        out_specs=[fixed, fixed, pl.BlockSpec((terms, tall, rows), lambda i: (0, 0, 0))],
        out_shape=[
            jax.ShapeDtypeStruct((tall, wide), jnp.float32),
            jax.ShapeDtypeStruct((tall, wide), jnp.float32),
            jax.ShapeDtypeStruct((terms, tall, rows), jnp.float32),
        ],
        scratch_shapes=[pltpu.VMEM((tall, wide), jnp.bfloat16)] * 2,
        compiler_params=pltpu.CompilerParams(vmem_limit_bytes=60 * 1024 * 1024),
    )(charge, weight, y, left, local)


def remote(source, target, sends, lands, place):
    return pltpu.make_async_remote_copy(
        src_ref=source,
        dst_ref=target,
        send_sem=sends,
        recv_sem=lands,
        device_id=place,
        device_id_type=pl.DeviceIdType.MESH,
    )


def greet(places):
    barrier = pltpu.get_barrier_semaphore()
    for place in places:
        pl.semaphore_signal(barrier, inc=1, device_id=place, device_id_type=pl.DeviceIdType.MESH)
    pl.semaphore_wait(barrier, len(places))


def gather_kernel(pack_ref, small_ref, ops_ref, smalls_ref, send_a, land_a, send_x, land_x, send_c, land_c, send_f, land_f, send_s, land_s, send_t, land_t, own):
    terms, bands = pack_ref.shape[:2]
    half = terms // 2
    me = lax.axis_index("terms")
    band = lax.axis_index("sect")
    twin = me + 1 - 2 * lax.rem(me, 2)
    near = band + 1 - 2 * lax.rem(band, 2)
    far = lax.rem(band + 2, 4)
    greet([(lax.rem(me + i, terms), band) for i in range(1, terms)] + [(me, near), (me, far)])
    keep = pltpu.make_async_copy(pack_ref.at[me], ops_ref.at[me], own.at[0])
    keep.start()
    keep_small = pltpu.make_async_copy(small_ref, smalls_ref.at[me], own.at[1])
    keep_small.start()
    first = []
    for i in range(1, terms):
        peer = lax.rem(me + i, terms)
        copy = remote(pack_ref.at[peer, band], ops_ref.at[me, band], send_a.at[i - 1], land_a.at[i - 1], (peer, band))
        copy.start()
        first.append(copy)
    tiny = []
    for i in range(half):
        place = (twin if i == 0 else lax.rem(me + 2 * i, terms), band)
        copy = remote(small_ref, smalls_ref.at[me], send_s.at[i], land_s.at[i], place)
        copy.start()
        tiny.append(copy)
    across, beside = [], []
    for i in range(1, terms):
        first[i - 1].wait_recv()
        block = ops_ref.at[lax.rem(me + terms - i, terms), band]
        copy = remote(block, block, send_x.at[i - 1], land_x.at[i - 1], (me, far))
        copy.start()
        across.append(copy)
        copy = remote(block, block, send_c.at[i - 1], land_c.at[i - 1], (me, near))
        copy.start()
        beside.append(copy)
    relay = []
    for i in range(1, half):
        tiny[i].wait_recv()
        block = smalls_ref.at[lax.rem(me + terms - 2 * i, terms)]
        copy = remote(block, block, send_t.at[i - 1], land_t.at[i - 1], (twin, band))
        copy.start()
        relay.append(copy)
    last = []
    for i in range(1, terms):
        across[i - 1].wait_recv()
        block = ops_ref.at[lax.rem(me + terms - i, terms), far]
        copy = remote(block, block, send_f.at[i - 1], land_f.at[i - 1], (me, near))
        copy.start()
        last.append(copy)
    for copy in beside + last + relay + tiny[:1]:
        copy.wait_recv()
    for copy in first + tiny + across + beside + relay + last:
        copy.wait_send()
    keep.wait()
    keep_small.wait()


def gather(pack, small):
    terms = pack.shape[0]
    vmem = pl.BlockSpec(memory_space=pltpu.VMEM)
    pair = [pltpu.SemaphoreType.DMA((terms - 1,))] * 2
    return pl.pallas_call(
        gather_kernel,
        in_specs=[vmem, vmem],
        out_specs=[vmem, vmem],
        out_shape=[
            jax.ShapeDtypeStruct(pack.shape, jnp.float32),
            jax.ShapeDtypeStruct((terms,) + small.shape, jnp.float32),
        ],
        scratch_shapes=pair * 6 + [pltpu.SemaphoreType.DMA((2,))],
        compiler_params=pltpu.CompilerParams(
            collective_id=0, has_side_effects=True, vmem_limit_bytes=40 * 1024 * 1024
        ),
    )(pack, small)


def finish_kernel(stay_ref, up_ref, part_ref, sigma_ref, new_ref, moved, got, send_a, land_a, edge):
    terms = part_ref.shape[0]
    me = lax.axis_index("terms")
    band = lax.axis_index("sect")
    bands = lax.axis_size("sect")
    upper = lax.rem(band + 1, bands)
    lower = lax.rem(band + bands - 1, bands)
    greet([(lax.rem(me + i, terms), band) for i in range(1, terms)] + [(me, upper), (me, lower)])
    shift = remote(up_ref, moved, edge.at[0], edge.at[1], (me, upper))
    shift.start()
    copies = []
    for i in range(1, terms):
        peer = lax.rem(me + i, terms)
        copy = remote(part_ref.at[peer], got.at[i - 1], send_a.at[i - 1], land_a.at[i - 1], (peer, band))
        copy.start()
        copies.append(copy)
    shift.wait()
    sigma_ref[...] = stay_ref[...] + jnp.where(band > 0, moved[...], 0.0)
    total = part_ref[me]
    for i, copy in enumerate(copies):
        copy.wait()
        total = total + got[i]
    new_ref[...] = total


def finish(stay, up, part):
    terms = part.shape[0]
    vmem = pl.BlockSpec(memory_space=pltpu.VMEM)
    return pl.pallas_call(
        finish_kernel,
        in_specs=[vmem] * 3,
        out_specs=[vmem] * 2,
        out_shape=[
            jax.ShapeDtypeStruct(stay.shape, jnp.float32),
            jax.ShapeDtypeStruct(part.shape[1:], jnp.float32),
        ],
        scratch_shapes=[
            pltpu.VMEM(stay.shape, jnp.float32),
            pltpu.VMEM((terms - 1,) + part.shape[1:], jnp.float32),
            pltpu.SemaphoreType.DMA((terms - 1,)),
            pltpu.SemaphoreType.DMA((terms - 1,)),
            pltpu.SemaphoreType.DMA((2,)),
        ],
        compiler_params=pltpu.CompilerParams(
            collective_id=1, has_side_effects=True, vmem_limit_bytes=40 * 1024 * 1024
        ),
    )(stay, up, part)


def body(wave, left, right, site, charge, source, coupling, owner):
    _, rows, phys, bond = wave.shape
    terms = lax.axis_size("terms")
    bands = lax.axis_size("sect")
    me = lax.axis_index("terms")
    cols = bond // terms
    per = LANES // cols
    pack = right[0].reshape(2, per, bond // per, terms, cols).transpose(3, 0, 2, 1, 4)
    pack = pack.reshape(terms, bands, -1, LANES)
    lines = site.size // LANES
    room = -lines % 8
    small = jnp.concatenate(
        (left[0].reshape(2 * rows, rows), site.reshape(lines, LANES), jnp.zeros((room, LANES), jnp.float32))
    )
    ops, smalls = gather(pack, small)
    sites = smalls[:, 2 * rows : 2 * rows + lines].reshape(terms // per, per, 2, phys, phys)
    weights = jnp.stack((sites[:, :, 0], sites[:, :, 1], sites[:, :, 0] + sites[:, :, 1]))
    slot = jnp.arange(LANES, dtype=jnp.int32) // cols
    coef = sum(jnp.where(slot == j, weights[:, :, j, :, :, None], 0.0) for j in range(per))
    y = act(wave.reshape(2, rows * phys, bond), ops.reshape(terms, 2, bond // per, LANES), coef, phys)
    local = lax.dynamic_slice_in_dim(wave, me * cols, cols, axis=3).reshape(2 * rows, phys * cols)
    term_ids = jnp.arange(terms, dtype=jnp.int32)
    hit = (source[:, :, None] == term_ids).astype(jnp.float32)
    place = (owner[None, :] == term_ids[:, None]).astype(jnp.float32)
    weight = jnp.sum(coupling[:, :, :, None] * hit, axis=2)
    weight = jnp.sum(place[None, :, :, None] * weight[:, None], axis=2)
    stay, up, part = close(charge, weight, y, smalls, local)
    sigma, new = finish(stay, up, part)
    return sigma.reshape(2, rows, phys, cols), new.reshape(1, 2, rows, rows)


def solution(mesh):
    placed = (
        P(None, "sect", None, None),
        P("terms", None, "sect", None),
        P("terms", None, None, None),
        P("terms", None, None, None),
        P(),
        P(),
        P(),
        P(),
    )
    return jax.shard_map(
        body,
        mesh=mesh,
        in_specs=placed,
        out_specs=(P(None, "sect", None, "terms"), P("terms", None, "sect", None)),
        check_vma=False,
    )
```

time: 219 us -> 141 us (0.64)
  Pallas kernels: 46.9 us -> 111 us
  waiting for transfers between devices: 60.3 us -> 0 us
  blocking collectives: 49.7 us -> 0 us
  between operations: 13.9 us -> 0.79 us
  local copies, waits for them, and re-layouts: 36.2 us -> 26.2 us
  matrix products: 4.23 us -> 0 us
    pallas_call x0 -> x2, Pallas kernels: none -> 61.1 us  [the longest x1 32.8 us: gather(): pl.pallas_call(gather_kernel, in_specs=[vmem, vmem], out_specs=[vmem, vme...]
    reduce_scatter x1 -> x0, waiting for transfers between devices: 57.4 us -> none  [body(): lax.psum_scatter(jnp.stack((n_re, n_im), 1), 'terms', scatter_dimension=0...]
    all_gather x1 -> x0, blocking collectives: 27.4 us -> none  [body(): sites = lax.all_gather(site, 'terms', axis=0, tiled=True)]
    all_to_all x1 -> x0, blocking collectives: 22.3 us -> none  [body(): lax.all_to_all(mine.reshape(2, part, terms, cols), 'terms', 2, 2, tiled=T...]
    unnamed x15 -> x24, local copies, waits for them, and re-layouts: 4.64 us -> 10.4 us
    another operation x4 -> x2, local copies, waits for them, and re-layouts: 7.92 us -> 2.57 us  [the longest x1 2.56 us: body(): right[0].reshape(2, per, bond // per, terms, cols).transpose(3, 0, 2, 1, 4)]
    slice x2, local copies, waits for them, and re-layouts: 4.54 us -> 0.01 us  [the longest x1 0.01 us: body(): sites[:, :, 1]]
    dot_general x8 -> x0, matrix products: 4.23 us -> none  [ein(): jnp.einsum(pattern, former, latter, precision=precision, preferred_elemen...]
  transfers between devices with their start and end apart: 4 -> 0, of which waited for: 2 -> 0; matrix products, arithmetic and copies ran while one was open for 13% -> 0% of each run, Pallas kernels for 0% -> 0%
where the time goes in v1:
time: 141 us
  Pallas kernels  111 us (79%)
  local copies, waits for them, and re-layouts  26.2 us (19%)
  other arithmetic  2.84 us (2%)
    pallas_call x1, Pallas kernels, act(): pl.pallas_call(act_kernel, grid=(rows // step,), in_specs=[pl.BlockSpec((...  35.1 us
    pallas_call x1, Pallas kernels, gather(): pl.pallas_call(gather_kernel, in_specs=[vmem, vmem], out_specs=[vmem, vme...  32.8 us
    pallas_call x1, Pallas kernels, finish(): pl.pallas_call(finish_kernel, in_specs=[vmem] * 3, out_specs=[vmem] * 2,...  28.4 us
    pallas_call x1, Pallas kernels, close(): pl.pallas_call(close_kernel, grid=(groups,), in_specs=[pl.BlockSpec(memor...  14.8 us
    unnamed x24, local copies, waits for them, and re-layouts  10.4 us
    reshape x2, local copies, waits for them, and re-layouts, body(): pack = pack.reshape(terms, bands, -1, LANES)  8.67 us

profile of v1, /device:TPU:12, one launch (start us, length us, event | category | flops | bytes accessed | tf_op | source)
XLA Modules:
  0.0 140.9 jit_solution(3158440096746301016)
XLA Ops:
  0.6 2.9 %copy.28 = f32[1,2,512,512]{2,3,1,0:T(8,128)} copy(f32[1,2,512,512]{3,2,1,0:T(8,128)} %param.10) | data formatting | bytes 4194304 | tf_op args[2]
  3.5 2.6 %reshape_squeeze.6 = f32[2,2,256,8,64]{2,1,4,3,0:T(2,128)S(1)} reshape(f32[1,2,512,512]{2,3,1,0:T(8,128)} %copy.28) | data formatting | bytes 4194304 | tf_op jit(solution)/shard_map/reshape;squeeze | solution.py:316
  6.1 4.3 %copy.37 = f32[8,2,256,2,64]{4,3,2,1,0:T(2,128)} copy(f32[8,2,256,2,64]{2,3,4,0,1:T(2,128)S(1)} %bitcast.28) | data formatting | bytes 4194304 | tf_op jit(solution)/shard_map/reshape | solution.py:317
  10.5 4.3 %reshape.84.pack_ref = f32[8,4,128,128]{3,2,1,0:T(8,128)S(1)} reshape(f32[8,2,256,2,64]{4,3,2,1,0:T(2,128)} %copy.37) | data formatting | bytes 4194304 | tf_op jit(solution)/shard_map/reshape | solution.py:317
  14.8 0.1 pad.5.clone
  14.9 0.0 copy-done.6
  14.9 0.1 reshape.78
  15.0 0.0 copy-done.5
  15.0 0.1 maximum_maximum_fusion.small_ref
  15.1 32.8 %shard_map.95 = (f32[8,4,128,128]{3,2,1,0:T(8,128)S(1)}, f32[8,264,128]{2,1,0:T(8,128)S(1)}) custom-call(f32[8,4,128,128]{3,2,1,0:T(8,128)S(1)} %reshape.84.pack_ref, f32[264,128]{1,0:T(8,128)S(1)} %maximum_maximum_fusion.small_ref), custom_call_target="tpu_custom_call" | custom-call | tf_op jit(solution)/shard_map/pallas_call | solution.py:245
  47.8 0.0 copy-start
  47.9 1.4 copy-done
  49.2 0.1 reshape.80
  49.4 1.9 %select_add_fusion.coef_ref = f32[3,4,16,16,128]{4,3,2,1,0:T(8,128)} fusion(f32[3,4,16,16]{3,2,1,0:T(8,128)S(1)} %get-tuple-element.23, f32[3,4,16,16]{3,2,1,0:T(8,128)S(1)} %get-tuple-element.22, pred[128]{0:T(512)(128)(4,1)S(1)} %get-tuple-element.29, pred[128]{0:T(512)(128)(4,1)S(1)} %get-tuple-element.28), kind=kLoop, calls=%fused_computation | loop fusion | flops 1179648 | bytes 1597696 | tf_op jit(solution)/shard_map/add | solution.py:327
  51.3 35.1 %shard_map.96.y_ref = f32[4,2,16,128,128]{4,3,2,1,0:T(8,128)} custom-call(f32[2,2048,512]{2,1,0:T(8,128)} %bitcast.27, f32[8,2,256,128]{3,2,1,0:T(8,128)} %bitcast.25, f32[3,4,16,16,128]{4,3,2,1,0:T(8,128)} %select_add_fusion.coef_ref), custom_call_target="tpu_custom_call" | custom-call | tf_op jit(solution)/shard_map/pallas_call | solution.py:75
  86.4 2.2 %constant_dynamic-slice_fusion = f32[2,128,16,64]{3,2,1,0:T(8,128)S(1)} fusion(f32[2,128,16,512]{3,2,1,0:T(8,128)} %param.8, s32[]{:T(128)S(6)} %select_n.20), kind=kLoop, calls=%fused_computation.18 | loop fusion | bytes 2097156 | tf_op jit(solution)/shard_map/dynamic_slice | solution.py:329
  88.6 0.0 copy-start.8
  88.6 0.0 copy-start.7
  88.6 0.0 copy-start.9
  88.6 1.5 %reshape.85.local_ref = f32[256,1024]{1,0:T(8,128)} reshape(f32[2,128,16,64]{3,2,1,0:T(8,128)S(1)} %constant_dynamic-slice_fusion) | data formatting | bytes 2097152 | tf_op jit(solution)/shard_map/reshape | solution.py:329
  90.2 0.0 copy-done.8
  90.2 0.1 fusion
  90.2 0.1 multiply_reduce_fusion.1
  90.3 0.7 multiply_reduce_fusion.weight_ref
  91.0 14.8 %shard_map.97 = (f32[256,1024]{1,0:T(8,128)}, f32[256,1024]{1,0:T(8,128)}, f32[8,256,128]{2,1,0:T(8,128)}) custom-call(s32[8]{0:T(128)} %charge_ref.1, f32[2,8,8]{2,1,0:T(8,128)} %multiply_reduce_fusion.weight_ref, f32[4,2,16,128,128]{4,3,2,1,0:T(8,128)} %shard_map.96.y_ref, f32[8,264,128]{2,1,0:T(8,128)} %copy-done.1, f32[256,1024]{1,0:T(8,128)} %reshape.85.local_ref), custom_call_target="tpu_custom_call" | custom-call | tf_op jit(solution)/shard_map/pallas_call | solution.py:145
  105.8 1.2 copy-done.2
  107.1 1.2 copy-done.3
  108.3 1.2 copy-done.4
  109.5 28.4 %shard_map.98 = (f32[256,1024]{1,0:T(8,128)S(1)}, f32[256,128]{1,0:T(8,128)S(1)}) custom-call(f32[256,1024]{1,0:T(8,128)S(1)} %copy-done.2, f32[256,1024]{1,0:T(8,128)S(1)} %copy-done.3, f32[8,256,128]{2,1,0:T(8,128)S(1)} %copy-done.4), custom_call_target="tpu_custom_call" | custom-call | tf_op jit(solution)/shard_map/pallas_call | solution.py:288
  137.9 0.6 reshape.86
  138.5 1.8 %copy.36 = f32[2,128,16,64]{1,3,2,0:T(8,128)} copy(f32[2,128,16,64]{3,2,1,0:T(8,128)S(1)} %reshape.86) | data formatting | bytes 2097152
  140.2 0.7 copy.51
  (19 shorter events, 0.1 us)
Async XLA Ops:
  10.5 4.4 %copy-start.6 = (f32[1,2,16,16]{3,2,1,0:T(8,128)S(1)}, f32[1,2,16,16]{3,2,1,0:T(8,128)}, u32[]{:S(2)}) copy-start(f32[1,2,16,16]{3,2,1,0:T(8,128)} %param.11) | copy-start | bytes 6148
  10.5 4.5 %copy-start.5 = (f32[1,2,128,128]{3,2,1,0:T(8,128)S(1)}, f32[1,2,128,128]{3,2,1,0:T(8,128)}, u32[]{:S(2)}) copy-start(f32[1,2,128,128]{3,2,1,0:T(8,128)} %param.9) | copy-start | bytes 393220
  47.8 1.4 copy-start
  49.2 37.2 %copy-start.1 = (f32[8,264,128]{2,1,0:T(8,128)}, f32[8,264,128]{2,1,0:T(8,128)S(1)}, u32[]{:S(2)}) copy-start(f32[8,264,128]{2,1,0:T(8,128)S(1)} %get-tuple-element.10.left_ref) | copy-start | bytes 3244036
  88.6 1.6 %copy-start.8 = (s32[8,3]{0,1:T(4,128)S(1)}, s32[8,3]{0,1:T(4,128)}, u32[]{:S(2)}) copy-start(s32[8,3]{0,1:T(4,128)} %param.13) | copy-start | bytes 292
  88.6 1.6 %copy-start.7 = (f32[2,8,3]{1,0,2:T(2,128)S(1)}, f32[2,8,3]{1,0,2:T(2,128)}, u32[]{:S(2)}) copy-start(f32[2,8,3]{1,0,2:T(2,128)} %param.14) | copy-start | bytes 580
  88.6 1.7 %copy-start.9 = (s32[8]{0:T(128)S(1)}, s32[8]{0:T(128)}, u32[]{:S(2)}) copy-start(s32[8]{0:T(128)} %param.15) | copy-start | bytes 100
  105.8 1.2 copy-start.2
  107.1 1.2 copy-start.3
  108.3 1.2 copy-start.4

commit v2 on v1

--- a/solution.py
+++ b/solution.py
@@ -87,7 +87,7 @@
             pltpu.VMEM((3, bond, width), jnp.bfloat16),
             pltpu.VMEM((3, groups, step * phys, LANES), jnp.float32),
         ],
-        compiler_params=pltpu.CompilerParams(vmem_limit_bytes=60 * 1024 * 1024),
+        compiler_params=pltpu.CompilerParams(vmem_limit_bytes=58 * 1024 * 1024),
     )(wave, ops, coef)
 
 
@@ -152,15 +152,38 @@
             pl.BlockSpec((per, lines, rows), lambda i: (i, 0, 0)),
             fixed,
         ],
-        out_specs=[fixed, fixed, pl.BlockSpec((terms, tall, rows), lambda i: (0, 0, 0))],
+        out_specs=[pl.BlockSpec(memory_space=pltpu.VMEM)] * 3,
         out_shape=[
             jax.ShapeDtypeStruct((tall, wide), jnp.float32),
             jax.ShapeDtypeStruct((tall, wide), jnp.float32),
             jax.ShapeDtypeStruct((terms, tall, rows), jnp.float32),
         ],
         scratch_shapes=[pltpu.VMEM((tall, wide), jnp.bfloat16)] * 2,
-        compiler_params=pltpu.CompilerParams(vmem_limit_bytes=60 * 1024 * 1024),
+        compiler_params=pltpu.CompilerParams(vmem_limit_bytes=54 * 1024 * 1024),
     )(charge, weight, y, left, local)
+
+
+def pack_kernel(right_ref, pack_ref):
+    terms, _, deep, _ = pack_ref.shape
+    cols = right_ref.shape[2] // terms
+    per = LANES // cols
+    for t in range(terms):
+        for h in range(2):
+            pieces = [right_ref[h, i * deep : (i + 1) * deep, t * cols : (t + 1) * cols] for i in range(per)]
+            pack_ref[t, h] = jnp.concatenate(pieces, axis=1)
+
+
+def packed(right, terms):
+    _, bond, width = right.shape
+    deep = bond * width // (terms * LANES)
+    vmem = pl.BlockSpec(memory_space=pltpu.VMEM)
+    return pl.pallas_call(
+        pack_kernel,
+        in_specs=[vmem],
+        out_specs=vmem,
+        out_shape=jax.ShapeDtypeStruct((terms, 2, deep, LANES), jnp.float32),
+        compiler_params=pltpu.CompilerParams(vmem_limit_bytes=16 * 1024 * 1024),
+    )(right)
 
 
 def remote(source, target, sends, lands, place):
@@ -252,12 +275,12 @@
         ],
         scratch_shapes=pair * 6 + [pltpu.SemaphoreType.DMA((2,))],
         compiler_params=pltpu.CompilerParams(
-            collective_id=0, has_side_effects=True, vmem_limit_bytes=40 * 1024 * 1024
+            collective_id=0, has_side_effects=True, vmem_limit_bytes=24 * 1024 * 1024
         ),
     )(pack, small)
 
 
-def finish_kernel(stay_ref, up_ref, part_ref, sigma_ref, new_ref, moved, got, send_a, land_a, edge):
+def finish_kernel(stay_ref, up_ref, part_ref, sigma_ref, new_ref, moved, got, held, mine, send_a, land_a, edge):
     terms = part_ref.shape[0]
     me = lax.axis_index("terms")
     band = lax.axis_index("sect")
@@ -273,9 +296,15 @@
         copy = remote(part_ref.at[peer], got.at[i - 1], send_a.at[i - 1], land_a.at[i - 1], (peer, band))
         copy.start()
         copies.append(copy)
+    keep = pltpu.make_async_copy(stay_ref, held, edge.at[2])
+    keep.start()
+    keep_part = pltpu.make_async_copy(part_ref.at[me], mine, edge.at[3])
+    keep_part.start()
+    keep.wait()
+    keep_part.wait()
     shift.wait()
-    sigma_ref[...] = stay_ref[...] + jnp.where(band > 0, moved[...], 0.0)
-    total = part_ref[me]
+    sigma_ref[...] = held[...] + jnp.where(band > 0, moved[...], 0.0)
+    total = mine[...]
     for i, copy in enumerate(copies):
         copy.wait()
         total = total + got[i]
@@ -287,7 +316,7 @@
     vmem = pl.BlockSpec(memory_space=pltpu.VMEM)
     return pl.pallas_call(
         finish_kernel,
-        in_specs=[vmem] * 3,
+        in_specs=[pl.BlockSpec(memory_space=pl.ANY)] * 3,
         out_specs=[vmem] * 2,
         out_shape=[
             jax.ShapeDtypeStruct(stay.shape, jnp.float32),
@@ -296,12 +325,14 @@
         scratch_shapes=[
             pltpu.VMEM(stay.shape, jnp.float32),
             pltpu.VMEM((terms - 1,) + part.shape[1:], jnp.float32),
+            pltpu.VMEM(stay.shape, jnp.float32),
+            pltpu.VMEM(part.shape[1:], jnp.float32),
             pltpu.SemaphoreType.DMA((terms - 1,)),
             pltpu.SemaphoreType.DMA((terms - 1,)),
-            pltpu.SemaphoreType.DMA((2,)),
+            pltpu.SemaphoreType.DMA((4,)),
         ],
         compiler_params=pltpu.CompilerParams(
-            collective_id=1, has_side_effects=True, vmem_limit_bytes=40 * 1024 * 1024
+            collective_id=1, has_side_effects=True, vmem_limit_bytes=24 * 1024 * 1024
         ),
     )(stay, up, part)
 
@@ -313,8 +344,7 @@
     me = lax.axis_index("terms")
     cols = bond // terms
     per = LANES // cols
-    pack = right[0].reshape(2, per, bond // per, terms, cols).transpose(3, 0, 2, 1, 4)
-    pack = pack.reshape(terms, bands, -1, LANES)
+    pack = packed(right[0], terms).reshape(terms, bands, -1, LANES)
     lines = site.size // LANES
     room = -lines % 8
     small = jnp.concatenate(

time: 141 us -> 129 us (0.915)
  local copies, waits for them, and re-layouts: 26.2 us -> 13.8 us
    reshape x2 -> x0, local copies, waits for them, and re-layouts: 8.67 us -> none  [body(): pack = pack.reshape(terms, bands, -1, LANES)]
    another operation x1 -> x0, local copies, waits for them, and re-layouts: 2.56 us -> none  [body(): right[0].reshape(2, per, bond // per, terms, cols).transpose(3, 0, 2, 1, 4)]
    unnamed x24 -> x25, local copies, waits for them, and re-layouts: 10.4 us -> 9.2 us
    pallas_call x1 -> x2, Pallas kernels: 28.4 us -> 29 us  [the longest x1 28.4 us: finish(): pl.pallas_call(finish_kernel, in_specs=[pl.BlockSpec(memory_space=pl.ANY)...]
where the time goes in v2:
time: 129 us
  Pallas kernels  112 us (87%)
  local copies, waits for them, and re-layouts  13.8 us (11%)
  other arithmetic  2.84 us (2%)
    pallas_call x1, Pallas kernels, act(): pl.pallas_call(act_kernel, grid=(rows // step,), in_specs=[pl.BlockSpec((...  35.1 us
    pallas_call x1, Pallas kernels, gather(): pl.pallas_call(gather_kernel, in_specs=[vmem, vmem], out_specs=[vmem, vme...  32.8 us
    pallas_call x1, Pallas kernels, finish(): pl.pallas_call(finish_kernel, in_specs=[pl.BlockSpec(memory_space=pl.ANY)...  28.4 us
    pallas_call x1, Pallas kernels, close(): pl.pallas_call(close_kernel, grid=(groups,), in_specs=[pl.BlockSpec(memor...  14.8 us
    unnamed x25, local copies, waits for them, and re-layouts  9.2 us

profile of v2, /device:TPU:12, one launch (start us, length us, event | category | flops | bytes accessed | tf_op | source)
XLA Modules:
  0.0 129.1 jit_solution(10022530437458870874)
XLA Ops:
  0.6 0.0 copy-start.1
  0.6 1.6 %copy-done.1 = f32[1,2,512,512]{3,2,1,0:T(8,128)S(1)} copy-done((f32[1,2,512,512]{3,2,1,0:T(8,128)S(1)}, f32[1,2,512,512]{3,2,1,0:T(8,128)}, u32[]{:S(2)}) %copy-start.1) | copy-done | bytes 2097176
  2.2 0.6 shard_map.95
  2.8 0.1 pad.5.clone
  2.9 0.0 copy-done.7
  2.9 0.1 reshape.78
  3.0 0.1 copy-done.6
  3.1 0.1 maximum_maximum_fusion.small_ref
  3.2 32.8 %shard_map.96 = (f32[8,4,128,128]{3,2,1,0:T(8,128)S(1)}, f32[8,264,128]{2,1,0:T(8,128)S(1)}) custom-call(f32[8,4,128,128]{3,2,1,0:T(8,128)S(1)} %bitcast.22, f32[264,128]{1,0:T(8,128)S(1)} %maximum_maximum_fusion.small_ref), custom_call_target="tpu_custom_call" | custom-call | tf_op jit(solution)/shard_map/pallas_call | solution.py:268
  36.0 0.0 copy-start
  36.0 1.4 %copy-done = f32[8,4,128,128]{3,2,1,0:T(8,128)} copy-done((f32[8,4,128,128]{3,2,1,0:T(8,128)}, f32[8,4,128,128]{3,2,1,0:T(8,128)S(1)}, u32[]{:S(2)}) %copy-start) | copy-done | bytes 2097176
  37.4 0.1 reshape.80
  37.6 1.9 %select_add_fusion.coef_ref = f32[3,4,16,16,128]{4,3,2,1,0:T(8,128)} fusion(f32[3,4,16,16]{3,2,1,0:T(8,128)S(1)} %get-tuple-element.23, f32[3,4,16,16]{3,2,1,0:T(8,128)S(1)} %get-tuple-element.22, pred[128]{0:T(512)(128)(4,1)S(1)} %get-tuple-element.29, pred[128]{0:T(512)(128)(4,1)S(1)} %get-tuple-element.28), kind=kLoop, calls=%fused_computation | loop fusion | flops 1179648 | bytes 1597696 | tf_op jit(solution)/shard_map/add | solution.py:357
  39.5 35.1 %shard_map.97.y_ref = f32[4,2,16,128,128]{4,3,2,1,0:T(8,128)} custom-call(f32[2,2048,512]{2,1,0:T(8,128)} %bitcast.26, f32[8,2,256,128]{3,2,1,0:T(8,128)} %bitcast.23, f32[3,4,16,16,128]{4,3,2,1,0:T(8,128)} %select_add_fusion.coef_ref), custom_call_target="tpu_custom_call" | custom-call | tf_op jit(solution)/shard_map/pallas_call | solution.py:75
  74.6 0.0 copy-done.2
  74.6 2.2 %constant_dynamic-slice_fusion = f32[2,128,16,64]{3,2,1,0:T(8,128)S(1)} fusion(f32[2,128,16,512]{3,2,1,0:T(8,128)} %param.8, s32[]{:T(128)S(6)} %select_n.20), kind=kLoop, calls=%fused_computation.18 | loop fusion | bytes 2097156 | tf_op jit(solution)/shard_map/dynamic_slice | solution.py:359
  76.8 0.0 copy-start.9
  76.8 0.0 copy-start.8
  76.8 0.0 copy-start.10
  76.8 1.5 %reshape.84.local_ref = f32[256,1024]{1,0:T(8,128)} reshape(f32[2,128,16,64]{3,2,1,0:T(8,128)S(1)} %constant_dynamic-slice_fusion) | data formatting | bytes 2097152 | tf_op jit(solution)/shard_map/reshape | solution.py:359
  78.4 0.0 copy-done.9
  78.4 0.1 fusion
  78.4 0.1 multiply_reduce_fusion.1
  78.5 0.7 multiply_reduce_fusion.weight_ref
  79.2 14.8 %shard_map.98 = (f32[256,1024]{1,0:T(8,128)}, f32[256,1024]{1,0:T(8,128)}, f32[8,256,128]{2,1,0:T(8,128)}) custom-call(s32[8]{0:T(128)} %charge_ref.1, f32[2,8,8]{2,1,0:T(8,128)} %multiply_reduce_fusion.weight_ref, f32[4,2,16,128,128]{4,3,2,1,0:T(8,128)} %shard_map.97.y_ref, f32[8,264,128]{2,1,0:T(8,128)} %copy-done.2, f32[256,1024]{1,0:T(8,128)} %reshape.84.local_ref), custom_call_target="tpu_custom_call" | custom-call | tf_op jit(solution)/shard_map/pallas_call | solution.py:145
  94.0 1.2 copy-done.3
  95.3 1.2 copy-done.4
  96.5 1.2 copy-done.5
  97.7 28.4 %shard_map.99 = (f32[256,1024]{1,0:T(8,128)S(1)}, f32[256,128]{1,0:T(8,128)S(1)}) custom-call(f32[256,1024]{1,0:T(8,128)S(1)} %copy-done.3, f32[256,1024]{1,0:T(8,128)S(1)} %copy-done.4, f32[8,256,128]{2,1,0:T(8,128)S(1)} %copy-done.5), custom_call_target="tpu_custom_call" | custom-call | tf_op jit(solution)/shard_map/pallas_call | solution.py:317
  126.1 0.6 reshape.85
  126.7 1.8 %copy.29 = f32[2,128,16,64]{1,3,2,0:T(8,128)} copy(f32[2,128,16,64]{3,2,1,0:T(8,128)S(1)} %reshape.85) | data formatting | bytes 2097152
  128.4 0.7 copy.42
  (18 shorter events, 0.1 us)
Async XLA Ops:
  0.6 1.6 %copy-start.1 = (f32[1,2,512,512]{3,2,1,0:T(8,128)S(1)}, f32[1,2,512,512]{3,2,1,0:T(8,128)}, u32[]{:S(2)}) copy-start(f32[1,2,512,512]{3,2,1,0:T(8,128)} %param.10) | copy-start | bytes 6291460
  2.2 0.7 copy-start.7
  2.2 0.9 copy-start.6
  36.0 1.4 %copy-start = (f32[8,4,128,128]{3,2,1,0:T(8,128)}, f32[8,4,128,128]{3,2,1,0:T(8,128)S(1)}, u32[]{:S(2)}) copy-start(f32[8,4,128,128]{3,2,1,0:T(8,128)S(1)} %get-tuple-element.9) | copy-start | bytes 6291460
  37.4 37.2 %copy-start.2 = (f32[8,264,128]{2,1,0:T(8,128)}, f32[8,264,128]{2,1,0:T(8,128)S(1)}, u32[]{:S(2)}) copy-start(f32[8,264,128]{2,1,0:T(8,128)S(1)} %get-tuple-element.10.left_ref) | copy-start | bytes 3244036
  76.8 1.6 %copy-start.9 = (s32[8,3]{0,1:T(4,128)S(1)}, s32[8,3]{0,1:T(4,128)}, u32[]{:S(2)}) copy-start(s32[8,3]{0,1:T(4,128)} %param.13) | copy-start | bytes 292
  76.8 1.6 %copy-start.8 = (f32[2,8,3]{1,0,2:T(2,128)S(1)}, f32[2,8,3]{1,0,2:T(2,128)}, u32[]{:S(2)}) copy-start(f32[2,8,3]{1,0,2:T(2,128)} %param.14) | copy-start | bytes 580
  76.8 1.7 %copy-start.10 = (s32[8]{0:T(128)S(1)}, s32[8]{0:T(128)}, u32[]{:S(2)}) copy-start(s32[8]{0:T(128)} %param.15) | copy-start | bytes 100
  94.0 1.2 copy-start.3
  95.3 1.2 copy-start.4
  96.5 1.2 copy-start.5
